TPU v7x, 128 devices: a whole 4x4x4 slice. The times are simulated.
128 devices in a mesh: pool: 32 (over x, z, core), exp: 4 (over y).
Axes of the slice: x: 4, y: 4, z: 4, core: 2. Of those that a mesh axis runs over, the one named last changes fastest.
Arguments:
- tokens: bfloat16 [512, 1024], P('pool'), as said below
- block_table: int32 [512, 128], replicated, may hold values from -1 to 4607, as said below
- lengths: int32 [512], replicated, may hold values from 1 to 16384, as said below
- k_cache: bfloat16 [4096, 128, 512], P('pool', None, 'exp'), as said below
- v_cache: bfloat16 [4096, 128, 512], P('pool', None, 'exp'), may hold values from -9 to 9
- hidden_store: bfloat16 [512, 128, 1024], P('pool'), may hold values from -6 to 6
- norm_attn: bfloat16 [1024], replicated, may hold values from 0.5 to 1.5
- w_query: bfloat16 [1024, 1024], P(None, 'exp'), as said below
- w_key: bfloat16 [1024, 512], P(None, 'exp'), may hold values from -0.1875 to 0.1875
- w_value: bfloat16 [1024, 512], P(None, 'exp'), may hold values from -0.1875 to 0.1875
- w_out: bfloat16 [1024, 1024], P('exp'), may hold values from -0.1875 to 0.1875
- norm_moe: bfloat16 [1024], replicated, may hold values from 0.5 to 1.5
- expert_ids: int32 [512, 8], P('pool'), may hold values from 0 to 31, all different within a row; in each aligned block of 16 rows (0 to 15, 16 to 31, ...) at most 8 rows name the same one
- gate_weights: float32 [512, 8], P('pool'), may hold values from 0.1 to 1
- w_gate: bfloat16 [32, 1024, 512], P('pool'), may hold values from -0.1875 to 0.1875
- w_up: bfloat16 [32, 1024, 512], P('pool'), may hold values from -0.1875 to 0.1875
- w_down: bfloat16 [32, 512, 1024], P('pool'), may hold values from -0.25 to 0.25
Outputs:
- layer_out: bfloat16 [512, 1024], P('pool', 'exp')
Inputs may be any that keep to these rules, and one draw needn't show every extreme that they name: `block_table`: every block number 0 to 4607 stands exactly once in the table; a request's blocks fill the start of its row and -1 fills the rest; each request has 1 to 128 blocks and some request has exactly 128. `lengths`: A request with n blocks has a length above (n - 1) * 128 and at most n * 128; some request has the length 16384. `expert_ids`: in the rows of one pool index no expert is named by more than 8 rows. `tokens`: entries lie within -8 to 8. `k_cache`: entries lie within -8 to 8. `w_query`: entries are of magnitude below 7 / sqrt(1024).
All inputs are finite; a program needn't handle non-finite values.
Results may differ from a plain program's by a relative error of at most 0.009.
Values may be sent and summed in bfloat16 or wider, within the bound.
No kernel may reach another device: no remote copies, remote signals or barrier semaphores. Data moves between devices by JAX's collectives and lax.ppermute only.
A program may use at most 128 MiB of HBM per device.

v0:
```python
import jax
import jax.numpy as jnp
from jax import lax
from jax.sharding import PartitionSpec as P

HEAD_SIZE = 64
NEG_FILL = -1e30
EPSILON = 1e-05
SCORE_SCALE = 0.125
HIGHEST = lax.Precision.HIGHEST


def merged(value, axis, join):
    pieces = jax.tree.map(lambda part: lax.all_gather(part, axis), value)
    head = jax.tree.map(lambda part: part[0], pieces)
    tail = jax.tree.map(lambda part: part[1:], pieces)
    so_far, _ = lax.scan(lambda so_far, piece: (join(so_far, piece), None), head, tail)
    return so_far


def rms_scale(row_vals, gain_row):
    mean_sq = jnp.mean(row_vals * row_vals, axis=-1, keepdims=True)
    return row_vals * lax.rsqrt(mean_sq + EPSILON) * gain_row


def merge_pair(first, second):
    top_a, sum_a, out_a = first
    top_b, sum_b, out_b = second
    row_top = jnp.maximum(top_a, top_b)
    weight_a = jnp.exp(top_a - row_top)
    weight_b = jnp.exp(top_b - row_top)
    spread = out_a.shape[-1] // top_a.shape[-1]
    merged_out = out_a * jnp.repeat(weight_a, spread, axis=-1) + out_b * jnp.repeat(
        weight_b, spread, axis=-1
    )
    return (row_top, sum_a * weight_a + sum_b * weight_b, merged_out)


def on_device(
    tokens,
    block_table,
    lengths,
    k_cache,
    v_cache,
    hidden_store,
    norm_attn,
    w_query,
    w_key,
    w_value,
    w_out,
    norm_moe,
    expert_ids,
    gate_weights,
    w_gate,
    w_up,
    w_down,
):
    pool_count = lax.axis_size("pool")
    exp_count = lax.axis_size("exp")
    pool_index = lax.axis_index("pool")
    exp_index = lax.axis_index("exp")
    req_dev = tokens.shape[0]
    model_width = tokens.shape[1]
    quarter = model_width // exp_count
    x_rows = tokens.astype(jnp.float32)
    normed = rms_scale(x_rows, norm_attn.astype(jnp.float32)).astype(jnp.bfloat16)
    queries = jnp.dot(normed, w_query, preferred_element_type=jnp.float32).astype(jnp.bfloat16)
    all_queries = lax.all_gather(queries, "pool", axis=0, tiled=True)
    stored_rows = hidden_store.reshape(-1, model_width)
    stored_shape = (hidden_store.shape[0], hidden_store.shape[1], w_key.shape[1])
    key_new = (
        jnp.dot(stored_rows, w_key, preferred_element_type=jnp.float32)
        .astype(jnp.bfloat16)
        .reshape(stored_shape)
    )
    value_new = (
        jnp.dot(stored_rows, w_value, preferred_element_type=jnp.float32)
        .astype(jnp.bfloat16)
        .reshape(stored_shape)
    )
    keys_here = jnp.concatenate([k_cache, key_new], axis=0)
    values_here = jnp.concatenate([v_cache, value_new], axis=0)
    slot_count, page_len, key_width = keys_here.shape
    query_width = queries.shape[1]
    kv_groups = key_width // HEAD_SIZE
    per_group = query_width // key_width
    head_count = query_width // HEAD_SIZE
    requests = block_table.shape[0]
    list_len = block_table.shape[1]
    flat_ids = block_table.reshape(-1)
    entry_index = jnp.arange(requests * list_len, dtype=jnp.int32)
    global_slot = pool_index * slot_count + jnp.arange(slot_count, dtype=jnp.int32)
    found_entry = jnp.sum(
        jnp.where(flat_ids[None, :] == global_slot[:, None], entry_index[None, :], 0), axis=1
    )
    slot_req = found_entry // list_len
    slot_block = found_entry % list_len
    member = slot_req[:, None] == jnp.arange(requests, dtype=jnp.int32)[None, :]
    member_low = member.astype(jnp.bfloat16)
    slot_queries = jnp.dot(member_low, all_queries, preferred_element_type=jnp.float32).astype(
        jnp.bfloat16
    )
    slot_length = jnp.sum(jnp.where(member, lengths[None, :], 0), axis=1)
    q_grouped = slot_queries.reshape(slot_count, kv_groups, per_group, HEAD_SIZE)
    k_grouped = keys_here.reshape(slot_count, page_len, kv_groups, HEAD_SIZE)
    v_grouped = values_here.reshape(slot_count, page_len, kv_groups, HEAD_SIZE)
    scores = (
        jnp.einsum("sgqd,stgd->sgqt", q_grouped, k_grouped, preferred_element_type=jnp.float32)
        * SCORE_SCALE
    )
    positions = slot_block[:, None] * page_len + jnp.arange(page_len, dtype=jnp.int32)[None, :]
    is_valid = (positions < slot_length[:, None])[:, None, None, :]
    masked = jnp.where(is_valid, scores, NEG_FILL)
    block_top = jnp.max(masked, axis=-1)
    weights = jnp.where(is_valid, jnp.exp(masked - block_top[..., None]), 0.0)
    block_sum = jnp.sum(weights, axis=-1)
    block_out = jnp.einsum(
        "sgqt,stgd->sgqd",
        weights.astype(jnp.bfloat16),
        v_grouped,
        preferred_element_type=jnp.float32,
    )
    slot_top = block_top.reshape(slot_count, head_count)
    slot_sum = block_sum.reshape(slot_count, head_count)
    slot_out = block_out.reshape(slot_count, query_width)
    local_top = jnp.max(jnp.where(member[:, :, None], slot_top[:, None, :], NEG_FILL), axis=0)
    own_top = jnp.max(jnp.where(member[:, :, None], local_top[None, :, :], NEG_FILL), axis=1)
    factor = jnp.exp(slot_top - own_top)
    one_hot = member.astype(jnp.float32)
    local_sum = jnp.einsum("sr,sh->rh", one_hot, slot_sum * factor, precision=HIGHEST)
    local_out = jnp.einsum(
        "sr,sc->rc", one_hot, slot_out * jnp.repeat(factor, HEAD_SIZE, axis=1), precision=HIGHEST
    )
    all_top, all_sum, all_out = merged((local_top, local_sum, local_out), "pool", merge_pair)
    row_start = pool_index * req_dev
    total_sum = lax.dynamic_slice_in_dim(all_sum, row_start, req_dev, 0)
    accum = lax.dynamic_slice_in_dim(all_out, row_start, req_dev, 0)
    attended = (accum / jnp.repeat(total_sum, HEAD_SIZE, axis=-1)).astype(jnp.bfloat16)
    projected = lax.psum(jnp.dot(attended, w_out, preferred_element_type=jnp.float32), "exp")
    mixed = x_rows + projected
    normed_moe = rms_scale(mixed, norm_moe.astype(jnp.float32)).astype(jnp.bfloat16)
    top_count = expert_ids.shape[1]
    capacity = min(req_dev, 2 * ((req_dev * top_count + pool_count - 1) // pool_count))
    route_flat = expert_ids.reshape(-1)
    expert_hit = (route_flat[:, None] == jnp.arange(pool_count, dtype=jnp.int32)[None, :]).astype(
        jnp.int32
    )
    slot_rank = jnp.sum(jnp.cumsum(expert_hit, axis=0) * expert_hit, axis=1) - 1
    slot_pos = route_flat * capacity + slot_rank
    placed = (
        slot_pos[:, None] == jnp.arange(pool_count * capacity, dtype=jnp.int32)[None, :]
    ).astype(jnp.float32)
    placed = placed.reshape(req_dev, top_count, pool_count * capacity)
    send_map = jnp.sum(placed, axis=1).astype(jnp.bfloat16)
    combine_map = jnp.einsum("tk,tkc->tc", gate_weights, placed, precision=HIGHEST)
    outgoing = jnp.einsum("tc,td->cd", send_map, normed_moe, preferred_element_type=jnp.float32)
    outgoing = outgoing.astype(jnp.bfloat16).reshape(pool_count, capacity, model_width)
    arrived = lax.all_to_all(outgoing, "pool", split_axis=0, concat_axis=0, tiled=True)
    sources = arrived.shape[0]
    slots_here = arrived.shape[1]
    row_block = arrived.reshape(-1, model_width)
    gate_act = jnp.dot(row_block, w_gate[0], preferred_element_type=jnp.float32)
    up_act = jnp.dot(row_block, w_up[0], preferred_element_type=jnp.float32)
    hidden = (jax.nn.silu(gate_act) * up_act).astype(jnp.bfloat16)
    expert_low = jnp.dot(hidden, w_down[0], preferred_element_type=jnp.float32).astype(jnp.bfloat16)
    expert_low = expert_low.reshape(sources, slots_here, model_width)
    expert_out = lax.dynamic_slice_in_dim(expert_low, exp_index * quarter, quarter, 2)
    returned = lax.all_to_all(expert_out, "pool", split_axis=0, concat_axis=0, tiled=True)
    moe_share = jnp.dot(
        combine_map,
        returned.reshape(pool_count * capacity, quarter).astype(jnp.float32),
        precision=HIGHEST,
    )
    mixed_share = lax.dynamic_slice_in_dim(mixed, exp_index * quarter, quarter, 1)
    return (mixed_share + moe_share).astype(jnp.bfloat16)


def solution(mesh):
    placed = (
        P("pool", None),
        P(),
        P(),
        P("pool", None, "exp"),
        P("pool", None, "exp"),
        P("pool", None, None),
        P(),
        P(None, "exp"),
        P(None, "exp"),
        P(None, "exp"),
        P("exp", None),
        P(),
        P("pool", None),
        P("pool", None),
        P("pool", None, None),
        P("pool", None, None),
        P("pool", None, None),
    )
    return jax.shard_map(
        on_device, mesh=mesh, in_specs=placed, out_specs=P("pool", "exp"), check_vma=False
    )
```

profile of v0, /device:TPU:1, one launch (start us, length us, event | category | flops | bytes accessed | tf_op | source)
XLA Modules:
  0.0 319.9 jit_solution(11277620771074689597)
XLA Ops:
  6.5 6.6 %select_reduce_fusion = s32[144]{0:T(256)S(1)} fusion(s32[65536]{0:T(1024)} %bitcast.87, s32[144]{0:T(256)S(1)} %iota_add_fusion), kind=kLoop, calls=%fused_computation.10 | loop fusion | flops 28311408 | bytes 263296 | tf_op jit(solution)/shard_map/reduce_sum | solution.py:93
  15.8 1.3 convolution_convert_fusion.5
  17.1 27.6 %all_gather.21 = bf16[512,256]{1,0:T(8,128)(2,1)S(1)} all-gather(bf16[16,256]{1,0:T(8,128)(2,1)S(1)} %convolution_convert_fusion.5), channel_id=1, replica_groups=mesh['pool'=32,'exp'=4] {'pool'}, dimensions={0}, use_global_device_ids=true | all-gather | bytes 270336 | tf_op jit(solution)/shard_map/all_gather | solution.py:68
  45.1 3.5 %convolution_convert_fusion.1 = bf16[2048,128]{1,0:T(8,128)(2,1)S(1)} fusion(bf16[2048,1024]{1,0:T(8,128)(2,1)} %bitcast.89, bf16[1024,128]{1,0:T(8,128)(2,1)} %param.27), kind=kOutput, calls=%fused_computation.20 | convolution fusion | flops 537133056 | bytes 4980736 | tf_op jit(solution)/shard_map/dot_general | solution.py:72
  49.6 6.4 %copy.75 = bf16[128,128,128]{1,2,0:T(8,128)(2,1)} copy(bf16[128,128,128]{2,1,0:T(8,128)(2,1)} %param.22) | data formatting | bytes 8388608 | tf_op args[3]
  56.1 3.7 %fusion.67 = (f32[144,2,2]{2,1,0:T(2,128)S(1)}, f32[144,2,2,128]{3,2,1,0:T(2,128)S(1)}) fusion(bf16[144,2,2,64]{3,2,1,0:T(2,128)(2,1)S(1)} %reshape.185, bf16[16,128,2,64]{1,3,2,0:T(8,128)(2,1)S(1)} %copy.77, bf16[128,128,2,64]{1,3,2,0:T(8,128)(2,1)} %bitcast.84, pred[144,128]{1,0:T(8,128)(4,1)S(1)} %add_compare_fusion), kind=kOutput, calls=%fused_computation.105 | convolution fusion | flops 12017088 | bytes 5107968 | tf_op jit(solution)/shard_map/sgqd,stgd->sgqt/dot_general | solution.py:108
  61.0 3.4 %convolution_convert_fusion = bf16[2048,128]{1,0:T(8,128)(2,1)S(1)} fusion(bf16[2048,1024]{1,0:T(8,128)(2,1)} %bitcast.90, bf16[1024,128]{1,0:T(8,128)(2,1)S(1)} %copy-done.6), kind=kOutput, calls=%fused_computation.19 | convolution fusion | flops 537133056 | bytes 4980736 | tf_op jit(solution)/shard_map/dot_general | solution.py:77
  65.5 6.4 %copy.80 = bf16[128,128,128]{1,2,0:T(8,128)(2,1)} copy(bf16[128,128,128]{2,1,0:T(8,128)(2,1)} %param.23) | data formatting | bytes 8388608 | tf_op args[4]
  71.9 4.8 %fusion.7 = f32[144,2,2,64]{3,2,1,0:T(2,128)S(1)} fusion(bf16[16,128,2,64]{1,3,2,0:T(8,128)(2,1)S(1)} %copy.82, bf16[128,128,2,64]{1,3,2,0:T(8,128)(2,1)} %bitcast.85, f32[144,2,2,128]{3,2,1,0:T(2,128)S(1)} %get-tuple-element.103, pred[144,128]{1,0:T(8,128)(4,1)S(1)} %add_compare_fusion, f32[144,2,2]{2,1,0:T(2,128)S(1)} %get-tuple-element.102), kind=kOutput, calls=%fused_computation.15 | convolution fusion | flops 12017664 | bytes 5181696 | tf_op jit(solution)/shard_map/sgqt,stgd->sgqd/dot_general | solution.py:117
  77.0 1.5 fusion.35
  79.9 24.3 %all-gather.1 = f32[16384,4]{0,1:T(4,128)S(1)} all-gather(f32[512,4]{0,1:T(4,128)S(1)} %fusion.36), channel_id=3, replica_groups=mesh['pool'=32,'exp'=4] {'pool'}, dimensions={0}, use_global_device_ids=true | all-gather | bytes 270336 | tf_op jit(solution)/shard_map/all_gather | solution.py:14
  104.3 22.6 %all-gather = f32[16384,4]{0,1:T(4,128)S(1)} all-gather(f32[512,4]{0,1:T(4,128)S(1)} %select_reduce_fusion.2), channel_id=2, replica_groups=mesh['pool'=32,'exp'=4] {'pool'}, dimensions={0}, use_global_device_ids=true | all-gather | bytes 270336 | tf_op jit(solution)/shard_map/all_gather | solution.py:14
  128.3 23.1 %all-gather.5.cloned.1.call-done = f32[16384,256]{1,0:T(8,128)} async-done(((f32[512,256]{1,0:T(8,128)}), f32[16384,256]{1,0:T(8,128)}) %all-gather.5.cloned.1.call-update) | async-done | bytes 16777232 | tf_op jit(solution)/shard_map/all_gather | solution.py:14
  152.7 11.1 %slice.35 = f32[15872,256]{1,0:T(8,128)} slice(f32[16384,256]{1,0:T(8,128)} %all-gather.5.cloned.1.call-done), slice={[512:16384], [0:256]} | slice | bytes 32505856 | tf_op jit(solution)/shard_map/slice | solution.py:16
  163.9 70.2 %while.14 = (s32[]{:T(128)}, f32[512,4]{0,1:T(4,128)S(1)}, f32[512,4]{0,1:T(4,128)S(1)}, f32[512,256]{0,1:T(8,128)S(1)}, f32[31,512,4]{1,2,0:T(4,128)}, /*index=...) while((s32[]{:T(128)}, f32[512,4]{0,1:T(4,128)S(1)}, f32[512,4]{0,1:T(4,128)S(1)}, ...), condition=%wide.region_8.9_spmd, body=%wide.region_7.8_spmd.sunk | while | flops 405506 | bytes 3752029 | solution.py:17
  173.7 1.1 constant_dynamic-slice_fusion.4
  182.8 1.1 constant_dynamic-slice_fusion.4
  185.0 1.1 constant_dynamic-slice_fusion.4
  194.1 1.1 constant_dynamic-slice_fusion.4
  196.4 1.1 constant_dynamic-slice_fusion.4
  205.4 1.1 constant_dynamic-slice_fusion.4
  216.7 1.1 constant_dynamic-slice_fusion.4
  225.8 1.1 constant_dynamic-slice_fusion.4
  228.0 1.1 constant_dynamic-slice_fusion.4
  235.3 37.8 %all-reduce.2.cloned.1.call-done = f32[16,1024]{1,0:T(8,128)} async-done(((f32[16,1024]{1,0:T(8,128)}), f32[16,1024]{1,0:T(8,128)}) %all-reduce.2.cloned.1.call-update) | async-done | bytes 65552 | tf_op jit(solution)/shard_map/psum | solution.py:139
  274.1 1.1 fusion.11
  275.2 9.7 %all-to-all-start = ((bf16[32,8,1024]{2,1,0:T(8,128)(2,1)}), bf16[32,8,1024]{2,1,0:T(8,128)(2,1)S(1)}, u32[]{:S(2)}, u32[]{:S(2)}) async-start(bf16[32,8,1024]{2,1,0:T(8,128)(2,1)} %fusion.11), calls=%async_computation | async-start | bytes 1048576 | tf_op jit(solution)/shard_map/all_to_all | solution.py:158
  285.0 11.5 %all-to-all-done = bf16[32,8,1024]{2,1,0:T(8,128)(2,1)S(1)} async-done(((bf16[32,8,1024]{2,1,0:T(8,128)(2,1)}), bf16[32,8,1024]{2,1,0:T(8,128)(2,1)S(1)}, u32[]{:S(2)}, u32[]{:S(2)}) %all-to-all-start) | async-done | bytes 524320 | tf_op jit(solution)/shard_map/all_to_all | solution.py:158
  296.5 1.7 fusion.20
  298.2 2.0 fusion.12
  300.9 3.6 %all-to-all-start.1 = ((bf16[32,8,256]{2,1,0:T(8,128)(2,1)}), bf16[32,8,256]{2,1,0:T(8,128)(2,1)S(1)}, u32[]{:S(2)}, u32[]{:S(2)}) async-start(bf16[32,8,256]{2,1,0:T(8,128)(2,1)} %constant_dynamic-slice_fusion.2), calls=%async_computation.1 | async-start | bytes 262144 | tf_op jit(solution)/shard_map/all_to_all | solution.py:168
  304.8 7.4 %all-to-all-done.1 = bf16[32,8,256]{2,1,0:T(8,128)(2,1)S(1)} async-done(((bf16[32,8,256]{2,1,0:T(8,128)(2,1)}), bf16[32,8,256]{2,1,0:T(8,128)(2,1)S(1)}, u32[]{:S(2)}, u32[]{:S(2)}) %all-to-all-start.1) | async-done | bytes 131104 | tf_op jit(solution)/shard_map/all_to_all | solution.py:168
  (185 shorter events, 74.2 us)
Async XLA Ops:
  6.5 291.6 %copy-start = (bf16[1,512,1024]{2,1,0:T(8,128)(2,1)S(1)}, bf16[1,512,1024]{2,1,0:T(8,128)(2,1)}, u32[]{:S(2)}) copy-start(bf16[1,512,1024]{2,1,0:T(8,128)(2,1)} %param.35) | copy-start | bytes 3145732
  6.5 144.9 %all-gather.5.cloned.1.call-start = ((), (), s32[]{:S(2)}) async-start(), calls=%async_computation.3 | async-start | bytes 17301504 | tf_op jit(solution)/shard_map/all_gather | solution.py:14
  56.1 4.9 %copy-start.6 = (bf16[1024,128]{1,0:T(8,128)(2,1)S(1)}, bf16[1024,128]{1,0:T(8,128)(2,1)}, u32[]{:S(2)}) copy-start(bf16[1024,128]{1,0:T(8,128)(2,1)} %param.28) | copy-start | bytes 786436
  76.7 50.9 %copy-start.3 = (s32[16,8]{0,1:T(8,128)S(1)}, s32[16,8]{0,1:T(8,128)}, u32[]{:S(2)}) copy-start(s32[16,8]{0,1:T(8,128)} %param.31) | copy-start | bytes 1540
  76.7 51.6 %copy-start.5 = (bf16[1024]{0:T(1024)(128)(2,1)S(1)}, bf16[1024]{0:T(1024)(128)(2,1)}, u32[]{:S(2)}) copy-start(bf16[1024]{0:T(1024)(128)(2,1)} %param.30) | copy-start | bytes 6148
  78.5 194.6 %all-reduce.2.cloned.1.call-start = ((), (), s32[]{:S(2)}) async-start(), calls=%async_computation.2 | async-start | bytes 131072 | tf_op jit(solution)/shard_map/psum | solution.py:139
  163.9 70.4 %copy-start.1 = (bf16[256,1024]{1,0:T(8,128)(2,1)S(1)}, bf16[256,1024]{1,0:T(8,128)(2,1)}, u32[]{:S(2)}) copy-start(bf16[256,1024]{1,0:T(8,128)(2,1)} %param.29) | copy-start | bytes 1572868
  163.9 109.2 %copy-start.2 = (bf16[16,1024]{1,0:T(8,128)(2,1)S(1)}, bf16[16,1024]{1,0:T(8,128)(2,1)}, u32[]{:S(2)}) copy-start(bf16[16,1024]{1,0:T(8,128)(2,1)} %param.19) | copy-start | bytes 98308
  163.9 121.0 %copy-start.4 = (f32[16,8]{0,1:T(8,128)S(1)}, f32[16,8]{0,1:T(8,128)}, u32[]{:S(2)}) copy-start(f32[16,8]{0,1:T(8,128)} %param.32) | copy-start | bytes 1540
  275.2 21.3 %all-to-all-start = ((bf16[32,8,1024]{2,1,0:T(8,128)(2,1)}), bf16[32,8,1024]{2,1,0:T(8,128)(2,1)S(1)}, u32[]{:S(2)}, u32[]{:S(2)}) async-start(bf16[32,8,1024]{2,1,0:T(8,128)(2,1)} %fusion.11), calls=%async_computation | async-start | bytes 1048576 | tf_op jit(solution)/shard_map/all_to_all | solution.py:158
  300.9 11.3 %all-to-all-start.1 = ((bf16[32,8,256]{2,1,0:T(8,128)(2,1)}), bf16[32,8,256]{2,1,0:T(8,128)(2,1)S(1)}, u32[]{:S(2)}, u32[]{:S(2)}) async-start(bf16[32,8,256]{2,1,0:T(8,128)(2,1)} %constant_dynamic-slice_fusion.2), calls=%async_computation.1 | async-start | bytes 262144 | tf_op jit(solution)/shard_map/all_to_all | solution.py:168
Sparse Core Ops, SparseCore 0:
  78.6 72.7 all-gather.4
  235.3 37.7 all-reduce.1
where the time goes:
time: 324 us; the launch traced here: 320 us
  waiting for transfers between devices  79.9 us (25%)
  blocking collectives  74.6 us (23%)
  local copies, waits for them, and re-layouts  70 us (22%)
  other arithmetic  42 us (13%)
  matrix products  25.4 us (8%)
  between operations  13.7 us (4%)
  starting transfers between devices  13.4 us (4%)
    all_gather x2, blocking collectives, merged(): pieces = jax.tree.map(lambda part: lax.all_gather(part, axis), value)  47 us
    dynamic_slice x62, local copies, waits for them, and re-layouts, merged(): lax.scan(lambda so_far, piece: (join(so_far, piece), None), head, tail)  39.6 us
    psum x1, waiting for transfers between devices, on_device(): lax.psum(jnp.dot(attended, w_out, preferred_element_type=jnp.float32), 'e...  37.8 us
    all_gather x1, blocking collectives, on_device(): all_queries = lax.all_gather(queries, 'pool', axis=0, tiled=True)  27.6 us
    all_gather x1, waiting for transfers between devices, merged(): pieces = jax.tree.map(lambda part: lax.all_gather(part, axis), value)  23.1 us
    add x31, other arithmetic, merge_pair(): return (row_top, sum_a * weight_a + sum_b * weight_b, merged_out)  22.5 us
    unnamed x18, local copies, waits for them, and re-layouts  13 us
    slice x3, local copies, waits for them, and re-layouts, merged(): tail = jax.tree.map(lambda part: part[1:], pieces)  11.9 us
  transfers between devices with their start and end apart: 4, of which 4 were waited for; matrix products, arithmetic and copies ran while one was open for 1% of the time, Pallas kernels for 0%

commit v1 on v0

--- a/solution.py
+++ b/solution.py
@@ -136,7 +136,9 @@
     total_sum = lax.dynamic_slice_in_dim(all_sum, row_start, req_dev, 0)
     accum = lax.dynamic_slice_in_dim(all_out, row_start, req_dev, 0)
     attended = (accum / jnp.repeat(total_sum, HEAD_SIZE, axis=-1)).astype(jnp.bfloat16)
-    projected = lax.psum(jnp.dot(attended, w_out, preferred_element_type=jnp.float32), "exp")
+    projected = jnp.sum(
+        lax.all_gather(jnp.dot(attended, w_out, preferred_element_type=jnp.float32), "exp"), axis=0
+    )
     mixed = x_rows + projected
     normed_moe = rms_scale(mixed, norm_moe.astype(jnp.float32)).astype(jnp.bfloat16)
     top_count = expert_ids.shape[1]

time: 324 us -> 292 us (0.901)
  waiting for transfers between devices: 79.9 us -> 42 us
  blocking collectives: 74.6 us -> 84.9 us
    psum x1 -> x0, waiting for transfers between devices: 37.8 us -> none  [on_device(): lax.psum(jnp.dot(attended, w_out, preferred_element_type=jnp.float32), 'e...]
    all_gather x0 -> x1, blocking collectives: none -> 10.3 us  [on_device(): lax.all_gather(jnp.dot(attended, w_out, preferred_element_type=jnp.float3...]
  transfers between devices with their start and end apart: 4 -> 3, of which waited for: 4 -> 3; matrix products, arithmetic and copies ran while one was open for 1% -> 1% of each run, Pallas kernels for 0% -> 0%
where the time goes in v1:
time: 292 us; the launch traced here: 289 us
  blocking collectives  84.9 us (29%)
  local copies, waits for them, and re-layouts  70 us (24%)
  waiting for transfers between devices  42 us (14%)
  other arithmetic  41.2 us (14%)
  matrix products  24.7 us (8%)
  between operations  13.7 us (5%)
  starting transfers between devices  11.3 us (4%)
    all_gather x2, blocking collectives, merged(): pieces = jax.tree.map(lambda part: lax.all_gather(part, axis), value)  47 us
    dynamic_slice x62, local copies, waits for them, and re-layouts, merged(): lax.scan(lambda so_far, piece: (join(so_far, piece), None), head, tail)  39.6 us
    all_gather x1, blocking collectives, on_device(): all_queries = lax.all_gather(queries, 'pool', axis=0, tiled=True)  27.6 us
    all_gather x1, waiting for transfers between devices, merged(): pieces = jax.tree.map(lambda part: lax.all_gather(part, axis), value)  23 us
    add x31, other arithmetic, merge_pair(): return (row_top, sum_a * weight_a + sum_b * weight_b, merged_out)  22.5 us
    unnamed x18, local copies, waits for them, and re-layouts  13 us
    slice x3, local copies, waits for them, and re-layouts, merged(): tail = jax.tree.map(lambda part: part[1:], pieces)  11.9 us
    all_to_all x1, waiting for transfers between devices, on_device(): lax.all_to_all(outgoing, 'pool', split_axis=0, concat_axis=0, tiled=True)  11.5 us
  transfers between devices with their start and end apart: 3, of which 3 were waited for; matrix products, arithmetic and copies ran while one was open for 1% of the time, Pallas kernels for 0%

profile of v1, /device:TPU:1, one launch (start us, length us, event | category | flops | bytes accessed | tf_op | source)
XLA Modules:
  0.0 288.7 jit_solution(3799352625239531753)
XLA Ops:
  6.5 6.6 %select_reduce_fusion = s32[144]{0:T(256)S(1)} fusion(s32[65536]{0:T(1024)} %bitcast.89, s32[144]{0:T(256)S(1)} %iota_add_fusion), kind=kLoop, calls=%fused_computation.10 | loop fusion | flops 28311408 | bytes 263296 | tf_op jit(solution)/shard_map/reduce_sum | solution.py:93
  15.8 1.3 convolution_convert_fusion.5
  17.1 27.6 %all_gather.27 = bf16[512,256]{1,0:T(8,128)(2,1)S(1)} all-gather(bf16[16,256]{1,0:T(8,128)(2,1)S(1)} %convolution_convert_fusion.5), channel_id=1, replica_groups=mesh['pool'=32,'exp'=4] {'pool'}, dimensions={0}, use_global_device_ids=true | all-gather | bytes 270336 | tf_op jit(solution)/shard_map/all_gather | solution.py:68
  45.1 3.5 %convolution_convert_fusion.1 = bf16[2048,128]{1,0:T(8,128)(2,1)S(1)} fusion(bf16[2048,1024]{1,0:T(8,128)(2,1)} %bitcast.91, bf16[1024,128]{1,0:T(8,128)(2,1)} %param.27), kind=kOutput, calls=%fused_computation.20 | convolution fusion | flops 537133056 | bytes 4980736 | tf_op jit(solution)/shard_map/dot_general | solution.py:72
  49.6 6.4 %copy.75 = bf16[128,128,128]{1,2,0:T(8,128)(2,1)} copy(bf16[128,128,128]{2,1,0:T(8,128)(2,1)} %param.22) | data formatting | bytes 8388608 | tf_op args[3]
  56.1 3.7 %fusion.67 = (f32[144,2,2]{2,1,0:T(2,128)S(1)}, f32[144,2,2,128]{3,2,1,0:T(2,128)S(1)}) fusion(bf16[144,2,2,64]{3,2,1,0:T(2,128)(2,1)S(1)} %reshape.185, bf16[16,128,2,64]{1,3,2,0:T(8,128)(2,1)S(1)} %copy.77, bf16[128,128,2,64]{1,3,2,0:T(8,128)(2,1)} %bitcast.85, pred[144,128]{1,0:T(8,128)(4,1)S(1)} %add_compare_fusion), kind=kOutput, calls=%fused_computation.105 | convolution fusion | flops 12017088 | bytes 5107968 | tf_op jit(solution)/shard_map/sgqd,stgd->sgqt/dot_general | solution.py:108
  61.0 3.4 %convolution_convert_fusion = bf16[2048,128]{1,0:T(8,128)(2,1)S(1)} fusion(bf16[2048,1024]{1,0:T(8,128)(2,1)} %bitcast.92, bf16[1024,128]{1,0:T(8,128)(2,1)S(1)} %copy-done.6), kind=kOutput, calls=%fused_computation.19 | convolution fusion | flops 537133056 | bytes 4980736 | tf_op jit(solution)/shard_map/dot_general | solution.py:77
  65.5 6.4 %copy.80 = bf16[128,128,128]{1,2,0:T(8,128)(2,1)} copy(bf16[128,128,128]{2,1,0:T(8,128)(2,1)} %param.23) | data formatting | bytes 8388608 | tf_op args[4]
  71.9 4.8 %fusion.7 = f32[144,2,2,64]{3,2,1,0:T(2,128)S(1)} fusion(bf16[16,128,2,64]{1,3,2,0:T(8,128)(2,1)S(1)} %copy.82, bf16[128,128,2,64]{1,3,2,0:T(8,128)(2,1)} %bitcast.86, f32[144,2,2,128]{3,2,1,0:T(2,128)S(1)} %get-tuple-element.103, pred[144,128]{1,0:T(8,128)(4,1)S(1)} %add_compare_fusion, f32[144,2,2]{2,1,0:T(2,128)S(1)} %get-tuple-element.102), kind=kOutput, calls=%fused_computation.15 | convolution fusion | flops 12017664 | bytes 5181696 | tf_op jit(solution)/shard_map/sgqt,stgd->sgqd/dot_general | solution.py:117
  77.0 1.5 fusion.35
  79.8 24.3 %all-gather.1 = f32[16384,4]{0,1:T(4,128)S(1)} all-gather(f32[512,4]{0,1:T(4,128)S(1)} %fusion.36), channel_id=3, replica_groups=mesh['pool'=32,'exp'=4] {'pool'}, dimensions={0}, use_global_device_ids=true | all-gather | bytes 270336 | tf_op jit(solution)/shard_map/all_gather | solution.py:14
  104.2 22.6 %all-gather = f32[16384,4]{0,1:T(4,128)S(1)} all-gather(f32[512,4]{0,1:T(4,128)S(1)} %select_reduce_fusion.2), channel_id=2, replica_groups=mesh['pool'=32,'exp'=4] {'pool'}, dimensions={0}, use_global_device_ids=true | all-gather | bytes 270336 | tf_op jit(solution)/shard_map/all_gather | solution.py:14
  128.4 23.0 %all-gather.6.cloned.1.call-done = f32[16384,256]{1,0:T(8,128)} async-done(((f32[512,256]{1,0:T(8,128)}), f32[16384,256]{1,0:T(8,128)}) %all-gather.6.cloned.1.call-update) | async-done | bytes 16777232 | tf_op jit(solution)/shard_map/all_gather | solution.py:14
  152.7 11.1 %slice.35 = f32[15872,256]{1,0:T(8,128)} slice(f32[16384,256]{1,0:T(8,128)} %all-gather.6.cloned.1.call-done), slice={[512:16384], [0:256]} | slice | bytes 32505856 | tf_op jit(solution)/shard_map/slice | solution.py:16
  163.8 70.2 %while.14 = (s32[]{:T(128)}, f32[512,4]{0,1:T(4,128)S(1)}, f32[512,4]{0,1:T(4,128)S(1)}, f32[512,256]{0,1:T(8,128)S(1)}, f32[31,512,4]{1,2,0:T(4,128)}, /*index=...) while((s32[]{:T(128)}, f32[512,4]{0,1:T(4,128)S(1)}, f32[512,4]{0,1:T(4,128)S(1)}, ...), condition=%wide.region_8.9_spmd, body=%wide.region_7.8_spmd.sunk | while | flops 405506 | bytes 3752029 | solution.py:17
  171.4 1.1 constant_dynamic-slice_fusion.4
  180.5 1.1 constant_dynamic-slice_fusion.4
  182.7 1.1 constant_dynamic-slice_fusion.4
  191.8 1.1 constant_dynamic-slice_fusion.4
  194.1 1.1 constant_dynamic-slice_fusion.4
  203.1 1.1 constant_dynamic-slice_fusion.4
  214.4 1.1 constant_dynamic-slice_fusion.4
  223.5 1.1 constant_dynamic-slice_fusion.4
  225.7 1.1 constant_dynamic-slice_fusion.4
  234.5 10.3 %all-gather.3 = f32[64,1024]{1,0:T(8,128)S(1)} all-gather(f32[16,1024]{1,0:T(8,128)S(1)} %fusion.68), channel_id=5, replica_groups=mesh['pool'=32,'exp'=4] {'exp'}, dimensions={0}, use_global_device_ids=true | all-gather | bytes 327680 | tf_op jit(solution)/shard_map/all_gather | solution.py:140
  245.0 1.1 fusion.11
  246.1 7.6 %all-to-all-start = ((bf16[32,8,1024]{2,1,0:T(8,128)(2,1)}), bf16[32,8,1024]{2,1,0:T(8,128)(2,1)S(1)}, u32[]{:S(2)}, u32[]{:S(2)}) async-start(bf16[32,8,1024]{2,1,0:T(8,128)(2,1)} %fusion.11), calls=%async_computation | async-start | bytes 1048576 | tf_op jit(solution)/shard_map/all_to_all | solution.py:160
  253.8 11.5 %all-to-all-done = bf16[32,8,1024]{2,1,0:T(8,128)(2,1)S(1)} async-done(((bf16[32,8,1024]{2,1,0:T(8,128)(2,1)}), bf16[32,8,1024]{2,1,0:T(8,128)(2,1)S(1)}, u32[]{:S(2)}, u32[]{:S(2)}) %all-to-all-start) | async-done | bytes 524320 | tf_op jit(solution)/shard_map/all_to_all | solution.py:160
  265.4 1.7 fusion.20
  267.0 2.0 fusion.12
  269.7 3.6 %all-to-all-start.1 = ((bf16[32,8,256]{2,1,0:T(8,128)(2,1)}), bf16[32,8,256]{2,1,0:T(8,128)(2,1)S(1)}, u32[]{:S(2)}, u32[]{:S(2)}) async-start(bf16[32,8,256]{2,1,0:T(8,128)(2,1)} %constant_dynamic-slice_fusion.2), calls=%async_computation.1 | async-start | bytes 262144 | tf_op jit(solution)/shard_map/all_to_all | solution.py:170
  273.7 7.4 %all-to-all-done.1 = bf16[32,8,256]{2,1,0:T(8,128)(2,1)S(1)} async-done(((bf16[32,8,256]{2,1,0:T(8,128)(2,1)}), bf16[32,8,256]{2,1,0:T(8,128)(2,1)S(1)}, u32[]{:S(2)}, u32[]{:S(2)}) %all-to-all-start.1) | async-done | bytes 131104 | tf_op jit(solution)/shard_map/all_to_all | solution.py:170
  (184 shorter events, 72.7 us)
Async XLA Ops:
  6.5 260.5 %copy-start = (bf16[1,512,1024]{2,1,0:T(8,128)(2,1)S(1)}, bf16[1,512,1024]{2,1,0:T(8,128)(2,1)}, u32[]{:S(2)}) copy-start(bf16[1,512,1024]{2,1,0:T(8,128)(2,1)} %param.35) | copy-start | bytes 3145732
  6.5 144.9 %all-gather.6.cloned.1.call-start = ((), (), s32[]{:S(2)}) async-start(), calls=%async_computation.2 | async-start | bytes 17301504 | tf_op jit(solution)/shard_map/all_gather | solution.py:14
  56.1 4.9 %copy-start.6 = (bf16[1024,128]{1,0:T(8,128)(2,1)S(1)}, bf16[1024,128]{1,0:T(8,128)(2,1)}, u32[]{:S(2)}) copy-start(bf16[1024,128]{1,0:T(8,128)(2,1)} %param.28) | copy-start | bytes 786436
  76.7 50.8 %copy-start.3 = (s32[16,8]{0,1:T(8,128)S(1)}, s32[16,8]{0,1:T(8,128)}, u32[]{:S(2)}) copy-start(s32[16,8]{0,1:T(8,128)} %param.31) | copy-start | bytes 1540
  76.7 51.5 %copy-start.5 = (bf16[1024]{0:T(1024)(128)(2,1)S(1)}, bf16[1024]{0:T(1024)(128)(2,1)}, u32[]{:S(2)}) copy-start(bf16[1024]{0:T(1024)(128)(2,1)} %param.30) | copy-start | bytes 6148
  163.8 70.4 %copy-start.1 = (bf16[256,1024]{1,0:T(8,128)(2,1)S(1)}, bf16[256,1024]{1,0:T(8,128)(2,1)}, u32[]{:S(2)}) copy-start(bf16[256,1024]{1,0:T(8,128)(2,1)} %param.29) | copy-start | bytes 1572868
  163.8 81.0 %copy-start.2 = (bf16[16,1024]{1,0:T(8,128)(2,1)S(1)}, bf16[16,1024]{1,0:T(8,128)(2,1)}, u32[]{:S(2)}) copy-start(bf16[16,1024]{1,0:T(8,128)(2,1)} %param.19) | copy-start | bytes 98308
  163.8 89.9 %copy-start.4 = (f32[16,8]{0,1:T(8,128)S(1)}, f32[16,8]{0,1:T(8,128)}, u32[]{:S(2)}) copy-start(f32[16,8]{0,1:T(8,128)} %param.32) | copy-start | bytes 1540
  246.1 19.3 %all-to-all-start = ((bf16[32,8,1024]{2,1,0:T(8,128)(2,1)}), bf16[32,8,1024]{2,1,0:T(8,128)(2,1)S(1)}, u32[]{:S(2)}, u32[]{:S(2)}) async-start(bf16[32,8,1024]{2,1,0:T(8,128)(2,1)} %fusion.11), calls=%async_computation | async-start | bytes 1048576 | tf_op jit(solution)/shard_map/all_to_all | solution.py:160
  269.7 11.3 %all-to-all-start.1 = ((bf16[32,8,256]{2,1,0:T(8,128)(2,1)}), bf16[32,8,256]{2,1,0:T(8,128)(2,1)S(1)}, u32[]{:S(2)}, u32[]{:S(2)}) async-start(bf16[32,8,256]{2,1,0:T(8,128)(2,1)} %constant_dynamic-slice_fusion.2), calls=%async_computation.1 | async-start | bytes 262144 | tf_op jit(solution)/shard_map/all_to_all | solution.py:170
Sparse Core Ops, SparseCore 0:
  78.6 72.7 all-gather.5
